TPU v7x, 32 devices: a whole 2x2x4 slice. The times are simulated.
32 devices in a mesh: region: 8 (over z, y), member: 4 (over x, core).
Axes of the slice: x: 2, y: 2, z: 4, core: 2. Of those that a mesh axis runs over, the one named last changes fastest.
Arguments:
- ensemble: bfloat16 [256, 16384], P('member', 'region'), may hold values from -6 to 6
- reports: float32 [8, 1024], P('region'), may hold values from -6 to 6
- report_count: int32 [8], P('region'), may hold values from 128 to 1024, as said below
- report_cell: int32 [8, 1024], P('region'), may hold values from 0 to 16383, as said below
- report_weight: float32 [8, 16, 1024], P('region', 'member'), may hold values from 0.001 to 1
- blending: float32 [4, 16384], P(None, ('region', 'member')), may hold values from 0.02 to 1
Outputs:
- analysis: bfloat16 [16384, 256], P(('region', 'member'))
Inputs may be any that keep to these rules, and one draw needn't show every extreme that they name: `report_count`: the largest value 1024 is reached by some region in every draw. `report_cell`: every cell lies in the slot's own region, or in the first 128 cells of one of at most two other regions chosen for that region.
All inputs are finite; a program needn't handle non-finite values.
Results may differ from a plain program's by a relative error of at most 0.0055.
Values may be sent and summed in bfloat16 or wider, within the bound.
No kernel may reach another device: no remote copies, remote signals or barrier semaphores. Data moves between devices by JAX's collectives and lax.ppermute only.
A program may use at most 64 MiB of HBM per device.

v0:
```python
import jax
import jax.numpy as jnp
from jax import lax
from jax.sharding import PartitionSpec as P

MARGIN = 128
SWEEPS = 4
highest = lax.Precision.HIGHEST


def extended(block, sides, width):
    for axis, dim in sides:
        count = lax.axis_size(axis)
        forward = [(i, i + 1) for i in range(count - 1)]
        backward = [(target, source) for source, target in forward]
        low = lax.ppermute(
            lax.slice_in_dim(block, block.shape[dim] - width, None, axis=dim), axis, forward
        )
        high = lax.ppermute(lax.slice_in_dim(block, 0, width, axis=dim), axis, backward)
        block = jnp.concatenate([low, block, high], axis=dim)
    return block


def make_transform(products, forcing, members):
    identity = jnp.eye(members, dtype=jnp.float32)
    precision_mat = (members - 1.0) * identity[None] + products
    frobenius = jnp.sqrt(jnp.sum(precision_mat * precision_mat, axis=(1, 2)))
    current = precision_mat / frobenius[:, None, None]
    root_iter = jnp.broadcast_to(identity, current.shape)
    for iteration in range(SWEEPS):
        middle = 1.5 * identity[None] - 0.5 * jnp.einsum(
            "aij,ajk->aik", root_iter, current, precision=highest
        )
        current = jnp.einsum("aij,ajk->aik", current, middle, precision=highest)
        root_iter = jnp.einsum("aij,ajk->aik", middle, root_iter, precision=highest)
    inverse_root = root_iter / jnp.sqrt(frobenius)[:, None, None]
    inner_step = jnp.einsum("aij,aj->ai", inverse_root, forcing, precision=highest)
    mean_weights = jnp.einsum("aij,aj->ai", inverse_root, inner_step, precision=highest)
    return (mean_weights[:, :, None] + jnp.sqrt(members - 1.0) * inverse_root).astype(jnp.bfloat16)


def corner_layout(band_index, points_here, row_count):
    group_index = jnp.arange(4 * points_here, dtype=jnp.int32)
    upper_half = group_index // (2 * points_here)
    column_block = group_index // 2 % points_here
    right_half = group_index % 2
    row_base = jnp.clip(band_index - 1 + upper_half, 0, row_count - 2)
    col_base = jnp.clip(column_block - 1 + right_half, 0, points_here - 2)
    return (row_base, col_base)


def per_device(ensemble, reports, report_count, report_cell, report_weight, blending):
    local_members, cell_count = ensemble.shape
    groups = lax.axis_size("member")
    members = local_members * groups
    region = lax.axis_index("region")
    member = lax.axis_index("member")
    targets = report_cell[0]
    holder = targets // cell_count
    within = targets % cell_count
    is_local = holder == region
    local_values = jnp.take(ensemble, jnp.where(is_local, within, 0), axis=1).astype(jnp.float32)
    border = ensemble[:, :MARGIN]
    border_index = holder * MARGIN + jnp.minimum(within, MARGIN - 1)
    pieces = lax.all_gather(border, "region", axis=1, tiled=True)
    extent = pieces.shape[1]
    inside = (border_index >= 0) & (border_index < extent) & jnp.logical_not(is_local)
    picked = jnp.take(pieces, jnp.clip(border_index, 0, extent - 1), axis=1).astype(jnp.float32)
    remote = jnp.where(inside[None, :], picked, 0.0)
    at_reports = jnp.where(is_local[None, :], local_values, remote)
    report_mean = lax.psum(jnp.sum(at_reports, axis=0), "member") / members
    local_pert = (at_reports - report_mean[None, :]).astype(jnp.bfloat16)
    report_pert = lax.all_gather(local_pert, "member", axis=0, tiled=True)
    active = (jnp.arange(report_pert.shape[1]) < report_count[0]).astype(jnp.float32)
    weights = report_weight[0] * active[None, :]
    weighted = (report_pert[None, :, :] * weights[:, None, :]).astype(jnp.bfloat16)
    departure = (weights * (reports[0] - report_mean)[None, :]).astype(jnp.bfloat16)
    products = jnp.einsum("ako,jo->akj", weighted, report_pert, preferred_element_type=jnp.float32)
    forcing = jnp.einsum("ao,ko->ak", departure, report_pert, preferred_element_type=jnp.float32)
    transform = make_transform(products, forcing, members)
    points_here = transform.shape[0]
    groups_band = 4 * points_here
    slab_cells = cell_count // groups
    group_cells = slab_cells // groups_band
    mixing = blending / jnp.sum(blending, axis=0, keepdims=True)
    columns = lax.all_to_all(ensemble, "member", split_axis=1, concat_axis=0, tiled=True)
    cell_mean = jnp.sum(columns, axis=0, dtype=jnp.float32) / members
    anomaly = (columns - cell_mean[None, :]).astype(jnp.bfloat16)
    anomaly_view = anomaly.reshape(members, groups_band, group_cells)
    mix_view = mixing.reshape(4, groups_band, group_cells)
    neighbours = extended(transform[None], (("member", 0),), 1)
    stacked = neighbours.reshape(3 * points_here, members, members)
    row_base, col_base = corner_layout(member, points_here, groups)
    running = jnp.zeros((groups_band, group_cells, members), jnp.float32)
    for corner in range(4):
        row_step = corner // 2
        col_step = corner % 2
        chosen_index = (row_base + row_step - (member - 1)) * points_here + col_base + col_step
        chosen = jnp.take(stacked, chosen_index, axis=0)
        spread = jnp.einsum(
            "kgc,gkj->gcj", anomaly_view, chosen, preferred_element_type=jnp.float32
        )
        running = running + mix_view[corner][:, :, None] * spread
    blended = running.reshape(slab_cells, members)
    return (cell_mean[:, None] + blended).astype(jnp.bfloat16)


def solution(mesh):
    return jax.shard_map(
        per_device,
        mesh=mesh,
        in_specs=(
            P("member", "region"),
            P("region", None),
            P("region"),
            P("region", None),
            P("region", "member", None),
            P(None, ("region", "member")),
        ),
        out_specs=P(("region", "member"), None),
        check_vma=False,
    )
```

profile of v0, /device:TPU:0, one launch (start us, length us, event | category | flops | bytes accessed | tf_op | source)
XLA Modules:
  0.0 104.7 jit_solution(4873198254214473473)
XLA Ops:
  1.6 1.2 %copy.24 = bf16[64,2048]{0,1:T(8,128)(2,1)S(1)} copy(bf16[64,2048]{1,0:T(8,128)(2,1)} %param.8) | data formatting | bytes 524288 | tf_op args[0]
  2.9 3.2 %gather_fusion = bf16[1024,64]{1,0:T(8,128)(2,1)S(1)} fusion(bf16[64,2048]{0,1:T(8,128)(2,1)S(1)} %copy.24, s32[1024]{0:T(1024)S(1)} %broadcast_clamp_fusion.1), kind=kCustom, calls=%fused_computation.4 | custom fusion | bytes 266240 | tf_op jit(solution)/shard_map/jit(_take)/gather | solution.py:62
  6.3 32.6 %all_gather.6 = bf16[64,1024]{0,1:T(8,128)(2,1)S(1)} all-gather(bf16[64,128]{0,1:T(8,128)(2,1)S(1)} %slice.37), channel_id=1, replica_groups=mesh['region'=8,'member'=4] {'region'}, dimensions={1}, use_global_device_ids=true | all-gather | bytes 147456 | tf_op jit(solution)/shard_map/all_gather | solution.py:65
  38.9 3.2 %gather_fusion.1 = bf16[1024,64]{1,0:T(8,128)(2,1)S(1)} fusion(bf16[64,1024]{0,1:T(8,128)(2,1)S(1)} %all_gather.6, s32[1024]{0:T(1024)S(1)} %broadcast_clamp_fusion), kind=kCustom, calls=%fused_computation.5 | custom fusion | bytes 266240 | tf_op jit(solution)/shard_map/jit(_take)/gather | solution.py:68
  42.3 5.7 %psum.7 = f32[1024]{0:T(1024)S(1)} all-reduce(f32[1024]{0:T(1024)S(1)} %fusion.54), channel_id=1, replica_groups=mesh['region'=8,'member'=4] {'member'}, use_global_device_ids=true, to_apply=%region_3.4 | all-reduce | flops 1024 | bytes 8192 | tf_op jit(solution)/shard_map/psum | solution.py:71
  48.1 7.4 %all_gather.7 = bf16[256,1024]{1,0:T(8,128)(2,1)S(1)} all-gather(bf16[64,1024]{1,0:T(8,128)(2,1)S(1)} %fusion.56), channel_id=1, replica_groups=mesh['region'=8,'member'=4] {'member'}, dimensions={0}, use_global_device_ids=true | all-gather | bytes 655360 | tf_op jit(solution)/shard_map/all_gather | solution.py:73
  57.2 1.2 %fusion.19 = f32[4,256,256]{2,1,0:T(8,128)S(1)} fusion(f32[256,256]{1,0:T(8,128)S(1)} %fusion.52, f32[256,256]{1,0:T(8,128)S(1)} %fusion.53, f32[4,256,256]{2,1,0:T(8,128)S(1)} %get-tuple-element.24, f32[4]{0:T(128)S(1)} %get-tuple-element.22), kind=kOutput, calls=%fused_computation.32 | convolution fusion | flops 806092800 | bytes 2621456 | tf_op jit(solution)/shard_map/aij,ajk->aik/dot_general | solution.py:31
  58.4 1.2 %fusion.55 = f32[4,256,256]{2,1,0:T(8,128)S(1)} fusion(f32[4,256,256]{2,1,0:T(8,128)S(1)} %fusion.19, f32[4,256,256]{2,1,0:T(8,128)S(1)} %get-tuple-element.24, f32[4]{0:T(128)S(1)} %get-tuple-element.22), kind=kOutput, calls=%fused_computation.66 | convolution fusion | flops 805568512 | bytes 3145744 | tf_op jit(solution)/shard_map/aij,ajk->aik/dot_general | solution.py:34
  60.7 1.2 %fusion.18 = f32[4,256,256]{2,1,0:T(8,128)S(1)} fusion(f32[4,256,256]{2,1,0:T(8,128)S(1)} %fusion.48, f32[4,256,256]{2,1,0:T(8,128)S(1)} %fusion.55, f32[256,256]{1,0:T(8,128)S(1)} %fusion.53), kind=kOutput, calls=%fused_computation.30 | convolution fusion | flops 805830656 | bytes 3407872 | tf_op jit(solution)/shard_map/aij,ajk->aik/dot_general | solution.py:31
  61.9 1.1 %fusion.79 = f32[4,256,256]{2,1,0:T(8,128)S(1)} fusion(f32[4,256,256]{2,1,0:T(8,128)S(1)} %fusion.55, f32[4,256,256]{2,1,0:T(8,128)S(1)} %fusion.18), kind=kOutput, calls=%fused_computation.158 | convolution fusion | flops 805306368 | bytes 3145728 | tf_op jit(solution)/shard_map/aij,ajk->aik/dot_general | solution.py:34
  63.0 1.1 %fusion.78 = f32[4,256,256]{2,1,0:T(8,128)S(1)} fusion(f32[4,256,256]{2,1,0:T(8,128)S(1)} %fusion.18, f32[4,256,256]{2,1,0:T(8,128)S(1)} %fusion.48), kind=kOutput, calls=%fused_computation.157 | convolution fusion | flops 805306368 | bytes 3145728 | tf_op jit(solution)/shard_map/aij,ajk->aik/dot_general | solution.py:35
  64.2 1.2 %fusion.17 = f32[4,256,256]{2,1,0:T(8,128)S(1)} fusion(f32[4,256,256]{2,1,0:T(8,128)S(1)} %fusion.78, f32[4,256,256]{2,1,0:T(8,128)S(1)} %fusion.79, f32[256,256]{1,0:T(8,128)S(1)} %fusion.53), kind=kOutput, calls=%fused_computation.28 | convolution fusion | flops 805830656 | bytes 3407872 | tf_op jit(solution)/shard_map/aij,ajk->aik/dot_general | solution.py:31
  65.4 1.1 %fusion.81 = f32[4,256,256]{2,1,0:T(8,128)S(1)} fusion(f32[4,256,256]{2,1,0:T(8,128)S(1)} %fusion.79, f32[4,256,256]{2,1,0:T(8,128)S(1)} %fusion.17), kind=kOutput, calls=%fused_computation.160 | convolution fusion | flops 805306368 | bytes 3145728 | tf_op jit(solution)/shard_map/aij,ajk->aik/dot_general | solution.py:34
  66.5 1.1 %fusion.80 = f32[4,256,256]{2,1,0:T(8,128)S(1)} fusion(f32[4,256,256]{2,1,0:T(8,128)S(1)} %fusion.17, f32[4,256,256]{2,1,0:T(8,128)S(1)} %fusion.78), kind=kOutput, calls=%fused_computation.159 | convolution fusion | flops 805306368 | bytes 3145728 | tf_op jit(solution)/shard_map/aij,ajk->aik/dot_general | solution.py:35
  67.9 1.4 %fusion.16 = f32[4,256,256]{2,1,0:T(8,128)S(1)} fusion(f32[4,256,256]{2,1,0:T(8,128)S(1)} %fusion.80, f32[4,256,256]{2,1,0:T(8,128)S(1)} %fusion.81, f32[256,256]{1,0:T(8,128)S(1)} %fusion.53), kind=kOutput, calls=%fused_computation.26 | convolution fusion | flops 805830656 | bytes 3407872 | tf_op jit(solution)/shard_map/aij,ajk->aik/dot_general | solution.py:31
  72.7 2.3 %collective-permute-start = (bf16[1,4,256,256]{3,2,1,0:T(8,128)(2,1)S(1)}, bf16[1,4,256,256]{3,2,1,0:T(8,128)(2,1)S(1)}, u32[]{:S(2)}, u32[]{:S(2)}) collective-permute-start(bf16[1,4,256,256]{3,2,1,0:T(8,128)(2,1)S(1)} %fusion.45), channel_id=1, source_target_pairs={{0,1},{1,2},{2,3},{4,5},{5,6},{6,7},{8,9},{9,10},{10,11},{12,13},{... | collective-permute-start | bytes 1572872 | tf_op jit(solution)/shard_map/ppermute | solution.py:16
  75.0 1.3 %collective-permute-start.1 = (bf16[1,4,256,256]{3,2,1,0:T(8,128)(2,1)S(1)}, bf16[1,4,256,256]{3,2,1,0:T(8,128)(2,1)S(1)}, u32[]{:S(2)}, u32[]{:S(2)}) collective-permute-start(bf16[1,4,256,256]{3,2,1,0:T(8,128)(2,1)S(1)} %fusion.45), channel_id=1, source_target_pairs={{1,0},{2,1},{3,2},{5,4},{6,5},{7,6},{9,8},{10,9},{11,10},{13,12},{... | collective-permute-start | bytes 1572872 | tf_op jit(solution)/shard_map/ppermute | solution.py:19
  77.0 4.1 %all-to-all-start = ((bf16[64,4,512]{2,0,1:T(8,128)(2,1)}), bf16[64,4,512]{2,0,1:T(8,128)(2,1)S(1)}, u32[]{:S(2)}, u32[]{:S(2)}) async-start(bf16[64,4,512]{2,0,1:T(8,128)(2,1)} %bitcast.73), calls=%async_computation | async-start | bytes 524288 | tf_op jit(solution)/shard_map/all_to_all | solution.py:86
  81.7 7.4 %all-to-all-done = bf16[64,4,512]{2,0,1:T(8,128)(2,1)S(1)} async-done(((bf16[64,4,512]{2,0,1:T(8,128)(2,1)}), bf16[64,4,512]{2,0,1:T(8,128)(2,1)S(1)}, u32[]{:S(2)}, u32[]{:S(2)}) %all-to-all-start) | async-done | bytes 262176 | tf_op jit(solution)/shard_map/all_to_all | solution.py:86
  90.7 2.0 %gather_fusion.3 = bf16[16,256,256]{2,1,0:T(8,128)(2,1)} fusion(bf16[12,256,256]{2,1,0:T(8,128)(2,1)S(1)} %bitcast.77, s32[1024]{0:T(1024)S(1)} %pad_clamp_fusion.2), kind=kCustom, calls=%fused_computation.1.clone | custom fusion | bytes 4194368 | tf_op jit(solution)/shard_map/jit(_take)/gather | solution.py:99
  92.7 2.0 %gather_fusion.4 = bf16[16,256,256]{2,1,0:T(8,128)(2,1)} fusion(bf16[12,256,256]{2,1,0:T(8,128)(2,1)S(1)} %bitcast.78, s32[1024]{0:T(1024)S(1)} %pad_clamp_fusion.1), kind=kCustom, calls=%fused_computation.2.clone | custom fusion | bytes 4194368 | tf_op jit(solution)/shard_map/jit(_take)/gather | solution.py:99
  94.7 2.0 %gather_fusion.5 = bf16[16,256,256]{2,1,0:T(8,128)(2,1)} fusion(bf16[12,256,256]{2,1,0:T(8,128)(2,1)S(1)} %bitcast.79, s32[1024]{0:T(1024)S(1)} %pad_clamp_fusion), kind=kCustom, calls=%fused_computation.3.clone | custom fusion | bytes 4194368 | tf_op jit(solution)/shard_map/jit(_take)/gather | solution.py:99
  96.7 2.0 %gather_fusion.2 = bf16[16,256,256]{2,1,0:T(8,128)(2,1)} fusion(bf16[12,256,256]{2,1,0:T(8,128)(2,1)S(1)} %bitcast.80, s32[1024]{0:T(1024)S(1)} %pad_clamp_fusion.3), kind=kCustom, calls=%fused_computation.clone | custom fusion | bytes 4194368 | tf_op jit(solution)/shard_map/jit(_take)/gather | solution.py:99
  98.7 2.3 %fusion.29 = f32[16,32,256]{2,1,0:T(8,128)S(1)} fusion(bf16[256,16,32]{0,2,1:T(8,128)(2,1)S(1)} %subtract_convert_fusion, bf16[16,256,256]{2,1,0:T(8,128)(2,1)} %gather_fusion.3, pred[16]{0:T(512)(128)(4,1)S(1)} %compare_and_fusion.4, f32[16,32]{1,0:T(8,128)S(1)} %mul.175), kind=kOutput, calls=%fused_computation.36 | convolution fusion | flops 68288512 | bytes 2885648 | tf_op jit(solution)/shard_map/kgc,gkj->gcj/dot_general | solution.py:100
  (76 shorter events, 14.2 us)
Async XLA Ops:
  0.0 6.2 %copy-start.4 = (s32[1,1024]{1,0:T(1,128)S(1)}, s32[1,1024]{1,0:T(1,128)}, u32[]{:S(2)}) copy-start(s32[1,1024]{1,0:T(1,128)} %param.11) | copy-start | bytes 12292
  2.9 45.1 %copy-start.7 = (f32[1,1024]{1,0:T(1,128)S(1)}, f32[1,1024]{1,0:T(1,128)}, u32[]{:S(2)}) copy-start(f32[1,1024]{1,0:T(1,128)} %param.9) | copy-start | bytes 12292
  38.9 17.5 %copy-start.6 = (f32[1,4,1024]{2,1,0:T(4,128)S(1)}, f32[1,4,1024]{2,1,0:T(4,128)}, u32[]{:S(2)}) copy-start(f32[1,4,1024]{2,1,0:T(4,128)} %param.12) | copy-start | bytes 49156
  70.5 5.8 %copy-start.3 = (bf16[64,2048]{1,0:T(8,128)(2,1)S(1)}, bf16[64,2048]{1,0:T(8,128)(2,1)}, u32[]{:S(2)}) copy-start(bf16[64,2048]{1,0:T(8,128)(2,1)} %param.8) | copy-start | bytes 786436
  71.5 9.8 %copy-start.5 = (f32[4,512]{1,0:T(4,128)S(1)}, f32[4,512]{1,0:T(4,128)}, u32[]{:S(2)}) copy-start(f32[4,512]{1,0:T(4,128)} %param.13) | copy-start | bytes 24580
  72.7 17.8 %collective-permute-start = (bf16[1,4,256,256]{3,2,1,0:T(8,128)(2,1)S(1)}, bf16[1,4,256,256]{3,2,1,0:T(8,128)(2,1)S(1)}, u32[]{:S(2)}, u32[]{:S(2)}) collective-permute-start(bf16[1,4,256,256]{3,2,1,0:T(8,128)(2,1)S(1)} %fusion.45), channel_id=1, source_target_pairs={{0,1},{1,2},{2,3},{4,5},{5,6},{6,7},{8,9},{9,10},{10,11},{12,13},{... | collective-permute-start | bytes 1572872 | tf_op jit(solution)/shard_map/ppermute | solution.py:16
  75.0 15.5 %collective-permute-start.1 = (bf16[1,4,256,256]{3,2,1,0:T(8,128)(2,1)S(1)}, bf16[1,4,256,256]{3,2,1,0:T(8,128)(2,1)S(1)}, u32[]{:S(2)}, u32[]{:S(2)}) collective-permute-start(bf16[1,4,256,256]{3,2,1,0:T(8,128)(2,1)S(1)} %fusion.45), channel_id=1, source_target_pairs={{1,0},{2,1},{3,2},{5,4},{6,5},{7,6},{9,8},{10,9},{11,10},{13,12},{... | collective-permute-start | bytes 1572872 | tf_op jit(solution)/shard_map/ppermute | solution.py:19
  77.0 12.1 %all-to-all-start = ((bf16[64,4,512]{2,0,1:T(8,128)(2,1)}), bf16[64,4,512]{2,0,1:T(8,128)(2,1)S(1)}, u32[]{:S(2)}, u32[]{:S(2)}) async-start(bf16[64,4,512]{2,0,1:T(8,128)(2,1)} %bitcast.73), calls=%async_computation | async-start | bytes 524288 | tf_op jit(solution)/shard_map/all_to_all | solution.py:86
  98.7 2.3 %copy-start.2 = (bf16[16,256,256]{2,1,0:T(8,128)(2,1)S(1)}, bf16[16,256,256]{2,1,0:T(8,128)(2,1)}, u32[]{:S(2)}) copy-start(bf16[16,256,256]{2,1,0:T(8,128)(2,1)} %gather_fusion.4) | copy-start | bytes 6291460
  101.0 1.6 %copy-start.1 = (bf16[16,256,256]{2,1,0:T(8,128)(2,1)S(1)}, bf16[16,256,256]{2,1,0:T(8,128)(2,1)}, u32[]{:S(2)}) copy-start(bf16[16,256,256]{2,1,0:T(8,128)(2,1)} %gather_fusion.5) | copy-start | bytes 6291460
  101.5 1.8 %copy-start = (bf16[16,256,256]{2,1,0:T(8,128)(2,1)S(1)}, bf16[16,256,256]{2,1,0:T(8,128)(2,1)}, u32[]{:S(2)}) copy-start(bf16[16,256,256]{2,1,0:T(8,128)(2,1)} %gather_fusion.2) | copy-start | bytes 6291460
where the time goes:
time: 105 us
  blocking collectives  45.6 us (43%)
  matrix products  19.8 us (19%)
  local copies, waits for them, and re-layouts  19.4 us (18%)
  starting transfers between devices  7.71 us (7%)
  waiting for transfers between devices  7.42 us (7%)
  other arithmetic  3.57 us (3%)
  between operations  1.12 us (1%)
    all_gather x1, blocking collectives, per_device(): pieces = lax.all_gather(border, 'region', axis=1, tiled=True)  32.6 us
    gather x4, local copies, waits for them, and re-layouts, per_device(): chosen = jnp.take(stacked, chosen_index, axis=0)  8.04 us
    all_to_all x1, waiting for transfers between devices, per_device(): lax.all_to_all(ensemble, 'member', split_axis=1, concat_axis=0, tiled=True)  7.41 us
    all_gather x1, blocking collectives, per_device(): report_pert = lax.all_gather(local_pert, 'member', axis=0, tiled=True)  7.41 us
    psum x1, blocking collectives, per_device(): report_mean = lax.psum(jnp.sum(at_reports, axis=0), 'member') / members  5.67 us
    dot_general x4, matrix products, make_transform(): jnp.einsum('aij,ajk->aik', root_iter, current, precision=highest)  4.92 us
    dot_general x4, matrix products, make_transform(): root_iter = jnp.einsum('aij,ajk->aik', middle, root_iter, precision=highest)  4.53 us
    all_to_all x1, starting transfers between devices, per_device(): lax.all_to_all(ensemble, 'member', split_axis=1, concat_axis=0, tiled=True)  4.14 us
  transfers between devices with their start and end apart: 3, of which 1 were waited for; matrix products, arithmetic and copies ran while one was open for 2% of the time, Pallas kernels for 0%

commit v1 on v0

--- a/solution.py
+++ b/solution.py
@@ -83,7 +83,12 @@
     slab_cells = cell_count // groups
     group_cells = slab_cells // groups_band
     mixing = blending / jnp.sum(blending, axis=0, keepdims=True)
-    columns = lax.all_to_all(ensemble, "member", split_axis=1, concat_axis=0, tiled=True)
+    columns = jnp.concatenate(
+        lax.all_to_all(
+            jnp.stack(jnp.split(ensemble, lax.axis_size("member"), axis=1)), "member", 0, 0
+        ),
+        axis=0,
+    )
     cell_mean = jnp.sum(columns, axis=0, dtype=jnp.float32) / members
     anomaly = (columns - cell_mean[None, :]).astype(jnp.bfloat16)
     anomaly_view = anomaly.reshape(members, groups_band, group_cells)

time: 105 us -> 106 us (level)
  other arithmetic: 3.57 us -> 5.3 us
where the time goes in v1:
time: 106 us
  blocking collectives  45.6 us (43%)
  matrix products  19.8 us (19%)
  local copies, waits for them, and re-layouts  18.6 us (18%)
  starting transfers between devices  7.72 us (7%)
  waiting for transfers between devices  7.38 us (7%)
  other arithmetic  5.3 us (5%)
  between operations  1.12 us (1%)
    all_gather x1, blocking collectives, per_device(): pieces = lax.all_gather(border, 'region', axis=1, tiled=True)  32.6 us
    gather x4, local copies, waits for them, and re-layouts, per_device(): chosen = jnp.take(stacked, chosen_index, axis=0)  8.04 us
    all_gather x1, blocking collectives, per_device(): report_pert = lax.all_gather(local_pert, 'member', axis=0, tiled=True)  7.41 us
    all_to_all x1, waiting for transfers between devices, per_device(): lax.all_to_all(jnp.stack(jnp.split(ensemble, lax.axis_size('member'), axi...  7.37 us
    psum x1, blocking collectives, per_device(): report_mean = lax.psum(jnp.sum(at_reports, axis=0), 'member') / members  5.67 us
    dot_general x4, matrix products, make_transform(): jnp.einsum('aij,ajk->aik', root_iter, current, precision=highest)  4.92 us
    dot_general x4, matrix products, make_transform(): root_iter = jnp.einsum('aij,ajk->aik', middle, root_iter, precision=highest)  4.53 us
    all_to_all x1, starting transfers between devices, per_device(): lax.all_to_all(jnp.stack(jnp.split(ensemble, lax.axis_size('member'), axi...  4.14 us
  transfers between devices with their start and end apart: 3, of which 1 were waited for; matrix products, arithmetic and copies ran while one was open for 2% of the time, Pallas kernels for 0%

profile of v1, /device:TPU:0, one launch (start us, length us, event | category | flops | bytes accessed | tf_op | source)
XLA Modules:
  0.0 105.6 jit_solution(17278711875546461227)
XLA Ops:
  1.6 1.2 %copy.13 = bf16[64,2048]{0,1:T(8,128)(2,1)S(1)} copy(bf16[64,2048]{1,0:T(8,128)(2,1)} %param.8) | data formatting | bytes 524288 | tf_op args[0]
  2.9 3.2 %gather_fusion = bf16[1024,64]{1,0:T(8,128)(2,1)S(1)} fusion(bf16[64,2048]{0,1:T(8,128)(2,1)S(1)} %copy.13, s32[1024]{0:T(1024)S(1)} %broadcast_clamp_fusion.1), kind=kCustom, calls=%fused_computation.4 | custom fusion | bytes 266240 | tf_op jit(solution)/shard_map/jit(_take)/gather | solution.py:62
  6.3 32.6 %all_gather.6 = bf16[64,1024]{0,1:T(8,128)(2,1)S(1)} all-gather(bf16[64,128]{0,1:T(8,128)(2,1)S(1)} %slice.37), channel_id=1, replica_groups=mesh['region'=8,'member'=4] {'region'}, dimensions={1}, use_global_device_ids=true | all-gather | bytes 147456 | tf_op jit(solution)/shard_map/all_gather | solution.py:65
  38.9 3.2 %gather_fusion.1 = bf16[1024,64]{1,0:T(8,128)(2,1)S(1)} fusion(bf16[64,1024]{0,1:T(8,128)(2,1)S(1)} %all_gather.6, s32[1024]{0:T(1024)S(1)} %broadcast_clamp_fusion), kind=kCustom, calls=%fused_computation.5 | custom fusion | bytes 266240 | tf_op jit(solution)/shard_map/jit(_take)/gather | solution.py:68
  42.3 5.7 %psum.7 = f32[1024]{0:T(1024)S(1)} all-reduce(f32[1024]{0:T(1024)S(1)} %fusion.54), channel_id=1, replica_groups=mesh['region'=8,'member'=4] {'member'}, use_global_device_ids=true, to_apply=%region_3.4 | all-reduce | flops 1024 | bytes 8192 | tf_op jit(solution)/shard_map/psum | solution.py:71
  48.1 7.4 %all_gather.7 = bf16[256,1024]{1,0:T(8,128)(2,1)S(1)} all-gather(bf16[64,1024]{1,0:T(8,128)(2,1)S(1)} %fusion.56), channel_id=1, replica_groups=mesh['region'=8,'member'=4] {'member'}, dimensions={0}, use_global_device_ids=true | all-gather | bytes 655360 | tf_op jit(solution)/shard_map/all_gather | solution.py:73
  57.2 1.2 %fusion.19 = f32[4,256,256]{2,1,0:T(8,128)S(1)} fusion(f32[256,256]{1,0:T(8,128)S(1)} %fusion.52, f32[256,256]{1,0:T(8,128)S(1)} %fusion.53, f32[4,256,256]{2,1,0:T(8,128)S(1)} %get-tuple-element.28, f32[4]{0:T(128)S(1)} %get-tuple-element.26), kind=kOutput, calls=%fused_computation.32 | convolution fusion | flops 806092800 | bytes 2621456 | tf_op jit(solution)/shard_map/aij,ajk->aik/dot_general | solution.py:31
  58.4 1.2 %fusion.55 = f32[4,256,256]{2,1,0:T(8,128)S(1)} fusion(f32[4,256,256]{2,1,0:T(8,128)S(1)} %fusion.19, f32[4,256,256]{2,1,0:T(8,128)S(1)} %get-tuple-element.28, f32[4]{0:T(128)S(1)} %get-tuple-element.26), kind=kOutput, calls=%fused_computation.64 | convolution fusion | flops 805568512 | bytes 3145744 | tf_op jit(solution)/shard_map/aij,ajk->aik/dot_general | solution.py:34
  60.7 1.2 %fusion.18 = f32[4,256,256]{2,1,0:T(8,128)S(1)} fusion(f32[4,256,256]{2,1,0:T(8,128)S(1)} %fusion.48, f32[4,256,256]{2,1,0:T(8,128)S(1)} %fusion.55, f32[256,256]{1,0:T(8,128)S(1)} %fusion.53), kind=kOutput, calls=%fused_computation.30 | convolution fusion | flops 805830656 | bytes 3407872 | tf_op jit(solution)/shard_map/aij,ajk->aik/dot_general | solution.py:31
  61.9 1.1 %fusion.79 = f32[4,256,256]{2,1,0:T(8,128)S(1)} fusion(f32[4,256,256]{2,1,0:T(8,128)S(1)} %fusion.55, f32[4,256,256]{2,1,0:T(8,128)S(1)} %fusion.18), kind=kOutput, calls=%fused_computation.161 | convolution fusion | flops 805306368 | bytes 3145728 | tf_op jit(solution)/shard_map/aij,ajk->aik/dot_general | solution.py:34
  63.0 1.1 %fusion.78 = f32[4,256,256]{2,1,0:T(8,128)S(1)} fusion(f32[4,256,256]{2,1,0:T(8,128)S(1)} %fusion.18, f32[4,256,256]{2,1,0:T(8,128)S(1)} %fusion.48), kind=kOutput, calls=%fused_computation.160 | convolution fusion | flops 805306368 | bytes 3145728 | tf_op jit(solution)/shard_map/aij,ajk->aik/dot_general | solution.py:35
  64.2 1.2 %fusion.17 = f32[4,256,256]{2,1,0:T(8,128)S(1)} fusion(f32[4,256,256]{2,1,0:T(8,128)S(1)} %fusion.78, f32[4,256,256]{2,1,0:T(8,128)S(1)} %fusion.79, f32[256,256]{1,0:T(8,128)S(1)} %fusion.53), kind=kOutput, calls=%fused_computation.28 | convolution fusion | flops 805830656 | bytes 3407872 | tf_op jit(solution)/shard_map/aij,ajk->aik/dot_general | solution.py:31
  65.4 1.1 %fusion.81 = f32[4,256,256]{2,1,0:T(8,128)S(1)} fusion(f32[4,256,256]{2,1,0:T(8,128)S(1)} %fusion.79, f32[4,256,256]{2,1,0:T(8,128)S(1)} %fusion.17), kind=kOutput, calls=%fused_computation.163 | convolution fusion | flops 805306368 | bytes 3145728 | tf_op jit(solution)/shard_map/aij,ajk->aik/dot_general | solution.py:34
  67.9 1.4 %fusion.16 = f32[4,256,256]{2,1,0:T(8,128)S(1)} fusion(f32[4,256,256]{2,1,0:T(8,128)S(1)} %fusion.80, f32[4,256,256]{2,1,0:T(8,128)S(1)} %fusion.81, f32[256,256]{1,0:T(8,128)S(1)} %fusion.53), kind=kOutput, calls=%fused_computation.26 | convolution fusion | flops 805830656 | bytes 3407872 | tf_op jit(solution)/shard_map/aij,ajk->aik/dot_general | solution.py:31
  72.7 2.3 %collective-permute-start = (bf16[1,4,256,256]{3,2,1,0:T(8,128)(2,1)S(1)}, bf16[1,4,256,256]{3,2,1,0:T(8,128)(2,1)S(1)}, u32[]{:S(2)}, u32[]{:S(2)}) collective-permute-start(bf16[1,4,256,256]{3,2,1,0:T(8,128)(2,1)S(1)} %fusion.45), channel_id=1, source_target_pairs={{0,1},{1,2},{2,3},{4,5},{5,6},{6,7},{8,9},{9,10},{10,11},{12,13},{... | collective-permute-start | bytes 1572872 | tf_op jit(solution)/shard_map/ppermute | solution.py:16
  75.0 1.3 %collective-permute-start.1 = (bf16[1,4,256,256]{3,2,1,0:T(8,128)(2,1)S(1)}, bf16[1,4,256,256]{3,2,1,0:T(8,128)(2,1)}, u32[]{:S(2)}, u32[]{:S(2)}) collective-permute-start(bf16[1,4,256,256]{3,2,1,0:T(8,128)(2,1)S(1)} %fusion.45), channel_id=1, source_target_pairs={{1,0},{2,1},{3,2},{5,4},{6,5},{7,6},{9,8},{10,9},{11,10},{13,12},{... | collective-permute-start | bytes 1572872 | tf_op jit(solution)/shard_map/ppermute | solution.py:19
  77.1 4.1 %all-to-all-start = ((bf16[4,64,512]{2,1,0:T(8,128)(2,1)}), bf16[4,64,512]{2,1,0:T(8,128)(2,1)S(1)}, u32[]{:S(2)}, u32[]{:S(2)}) async-start(bf16[4,64,512]{2,1,0:T(8,128)(2,1)} %pad_maximum_fusion.1), calls=%async_computation | async-start | bytes 524288 | tf_op jit(solution)/shard_map/all_to_all | solution.py:87
  81.7 7.4 %all-to-all-done = bf16[4,64,512]{2,1,0:T(8,128)(2,1)S(1)} async-done(((bf16[4,64,512]{2,1,0:T(8,128)(2,1)}), bf16[4,64,512]{2,1,0:T(8,128)(2,1)S(1)}, u32[]{:S(2)}, u32[]{:S(2)}) %all-to-all-start) | async-done | bytes 262176 | tf_op jit(solution)/shard_map/all_to_all | solution.py:87
  90.3 1.2 %pad_maximum_fusion = bf16[3,4,256,256]{3,2,1,0:T(8,128)(2,1)S(1)} fusion(bf16[1,4,256,256]{3,2,1,0:T(8,128)(2,1)} %collective-permute-done.1, bf16[1,4,256,256]{3,2,1,0:T(8,128)(2,1)S(1)} %fusion.45, bf16[1,4,256,256]{3,2,1,0:T(8,128)(2,1)S(1)} %collective-permute-done), kind=kLoop, calls=%fused_computation.22 | loop fusion | flops 1572864 | bytes 3145728 | tf_op jit(solution)/shard_map/concatenate | solution.py:20
  91.6 2.0 %gather_fusion.4 = bf16[16,256,256]{2,1,0:T(8,128)(2,1)} fusion(bf16[12,256,256]{2,1,0:T(8,128)(2,1)S(1)} %bitcast.79, s32[1024]{0:T(1024)S(1)} %pad_clamp_fusion.1), kind=kCustom, calls=%fused_computation.2.clone | custom fusion | bytes 4194368 | tf_op jit(solution)/shard_map/jit(_take)/gather | solution.py:104
  93.5 2.0 %gather_fusion.3 = bf16[16,256,256]{2,1,0:T(8,128)(2,1)} fusion(bf16[12,256,256]{2,1,0:T(8,128)(2,1)S(1)} %bitcast.80, s32[1024]{0:T(1024)S(1)} %pad_clamp_fusion.2), kind=kCustom, calls=%fused_computation.1.clone | custom fusion | bytes 4194368 | tf_op jit(solution)/shard_map/jit(_take)/gather | solution.py:104
  95.5 2.0 %gather_fusion.5 = bf16[16,256,256]{2,1,0:T(8,128)(2,1)} fusion(bf16[12,256,256]{2,1,0:T(8,128)(2,1)S(1)} %bitcast.81, s32[1024]{0:T(1024)S(1)} %pad_clamp_fusion), kind=kCustom, calls=%fused_computation.3.clone | custom fusion | bytes 4194368 | tf_op jit(solution)/shard_map/jit(_take)/gather | solution.py:104
  97.6 2.0 %gather_fusion.2 = bf16[16,256,256]{2,1,0:T(8,128)(2,1)} fusion(bf16[12,256,256]{2,1,0:T(8,128)(2,1)S(1)} %bitcast.82, s32[1024]{0:T(1024)S(1)} %pad_clamp_fusion.3), kind=kCustom, calls=%fused_computation.clone | custom fusion | bytes 4194368 | tf_op jit(solution)/shard_map/jit(_take)/gather | solution.py:104
  99.6 2.3 %fusion.32 = f32[16,32,256]{2,1,0:T(8,128)S(1)} fusion(bf16[256,16,32]{0,2,1:T(8,128)(2,1)S(1)} %subtract_convert_fusion, bf16[16,256,256]{2,1,0:T(8,128)(2,1)} %gather_fusion.4, pred[16]{0:T(512)(128)(4,1)S(1)} %get-tuple-element.34, f32[16,32]{1,0:T(8,128)S(1)} %mul.178), kind=kOutput, calls=%fused_computation.37 | convolution fusion | flops 68288512 | bytes 2885648 | tf_op jit(solution)/shard_map/kgc,gkj->gcj/dot_general | solution.py:105
  (76 shorter events, 15.1 us)
Async XLA Ops:
  0.0 6.2 %copy-start.4 = (s32[1,1024]{1,0:T(1,128)S(1)}, s32[1,1024]{1,0:T(1,128)}, u32[]{:S(2)}) copy-start(s32[1,1024]{1,0:T(1,128)} %param.11) | copy-start | bytes 12292
  2.9 45.1 %copy-start.7 = (f32[1,1024]{1,0:T(1,128)S(1)}, f32[1,1024]{1,0:T(1,128)}, u32[]{:S(2)}) copy-start(f32[1,1024]{1,0:T(1,128)} %param.9) | copy-start | bytes 12292
  38.9 17.5 %copy-start.6 = (f32[1,4,1024]{2,1,0:T(4,128)S(1)}, f32[1,4,1024]{2,1,0:T(4,128)}, u32[]{:S(2)}) copy-start(f32[1,4,1024]{2,1,0:T(4,128)} %param.12) | copy-start | bytes 49156
  70.5 5.8 %copy-start.3 = (bf16[64,2048]{1,0:T(8,128)(2,1)S(1)}, bf16[64,2048]{1,0:T(8,128)(2,1)}, u32[]{:S(2)}) copy-start(bf16[64,2048]{1,0:T(8,128)(2,1)} %param.8) | copy-start | bytes 786436
  71.5 9.8 %copy-start.5 = (f32[4,512]{1,0:T(4,128)S(1)}, f32[4,512]{1,0:T(4,128)}, u32[]{:S(2)}) copy-start(f32[4,512]{1,0:T(4,128)} %param.13) | copy-start | bytes 24580
  72.7 17.6 %collective-permute-start = (bf16[1,4,256,256]{3,2,1,0:T(8,128)(2,1)S(1)}, bf16[1,4,256,256]{3,2,1,0:T(8,128)(2,1)S(1)}, u32[]{:S(2)}, u32[]{:S(2)}) collective-permute-start(bf16[1,4,256,256]{3,2,1,0:T(8,128)(2,1)S(1)} %fusion.45), channel_id=1, source_target_pairs={{0,1},{1,2},{2,3},{4,5},{5,6},{6,7},{8,9},{9,10},{10,11},{12,13},{... | collective-permute-start | bytes 1572872 | tf_op jit(solution)/shard_map/ppermute | solution.py:16
  75.0 15.3 %collective-permute-start.1 = (bf16[1,4,256,256]{3,2,1,0:T(8,128)(2,1)S(1)}, bf16[1,4,256,256]{3,2,1,0:T(8,128)(2,1)}, u32[]{:S(2)}, u32[]{:S(2)}) collective-permute-start(bf16[1,4,256,256]{3,2,1,0:T(8,128)(2,1)S(1)} %fusion.45), channel_id=1, source_target_pairs={{1,0},{2,1},{3,2},{5,4},{6,5},{7,6},{9,8},{10,9},{11,10},{13,12},{... | collective-permute-start | bytes 1572872 | tf_op jit(solution)/shard_map/ppermute | solution.py:19
  77.1 12.0 %all-to-all-start = ((bf16[4,64,512]{2,1,0:T(8,128)(2,1)}), bf16[4,64,512]{2,1,0:T(8,128)(2,1)S(1)}, u32[]{:S(2)}, u32[]{:S(2)}) async-start(bf16[4,64,512]{2,1,0:T(8,128)(2,1)} %pad_maximum_fusion.1), calls=%async_computation | async-start | bytes 524288 | tf_op jit(solution)/shard_map/all_to_all | solution.py:87
  99.6 2.3 %copy-start.2 = (bf16[16,256,256]{2,1,0:T(8,128)(2,1)S(1)}, bf16[16,256,256]{2,1,0:T(8,128)(2,1)}, u32[]{:S(2)}) copy-start(bf16[16,256,256]{2,1,0:T(8,128)(2,1)} %gather_fusion.3) | copy-start | bytes 6291460
  101.9 1.6 %copy-start.1 = (bf16[16,256,256]{2,1,0:T(8,128)(2,1)S(1)}, bf16[16,256,256]{2,1,0:T(8,128)(2,1)}, u32[]{:S(2)}) copy-start(bf16[16,256,256]{2,1,0:T(8,128)(2,1)} %gather_fusion.5) | copy-start | bytes 6291460
  102.4 1.8 %copy-start = (bf16[16,256,256]{2,1,0:T(8,128)(2,1)S(1)}, bf16[16,256,256]{2,1,0:T(8,128)(2,1)}, u32[]{:S(2)}) copy-start(bf16[16,256,256]{2,1,0:T(8,128)(2,1)} %gather_fusion.2) | copy-start | bytes 6291460
